TPU v7x, 256 devices: a whole 4x4x8 slice. The times are simulated.
256 devices in a mesh: row: 8 (over x, y_lo), col: 32 (over y_hi, z, core).
Axes of the slice: x: 4, y: 4 (y_hi: 2, y_lo: 2; y = y_hi * 2 + y_lo), z: 8, core: 2. Of those that a mesh axis runs over, the one named last changes fastest.
Arguments:
- saved_inverse: float32 [4, 8, 512, 1, 32, 512], P(None, 'row', None, None, 'col'), may hold values from -0.046875 to 0.046875
- inverse_adjoint: float32 [4, 8, 512, 1, 32, 512], P(None, 'row', None, None, 'col'), may hold values from -6 to 6
Outputs:
- panel_adjoint: float32 [1024, 1, 32, 512], P('row', None, 'col')
All inputs are finite; a program needn't handle non-finite values.
Results may differ from a plain program's by a relative error of at most 0.000084.
Values sent between devices are 32-bit elements; how exact they have to be, the bound alone decides.
No kernel may reach another device: no remote copies, remote signals or barrier semaphores. Data moves between devices by JAX's collectives and lax.ppermute only.
A program may use at most 128 MiB of HBM per device.

v0:
```python
import jax
import jax.numpy as jnp
from jax import lax
from jax.sharding import PartitionSpec as P

M = 16384
K = 1024


def per_device(saved_inverse, inverse_adjoint):
    row_count = lax.axis_size("row")
    col_count = lax.axis_size("col")
    row_at = lax.axis_index("row")
    col_at = lax.axis_index("col")
    tiles_r = saved_inverse.shape[0]
    tile_size = saved_inverse.shape[2]
    tiles_c = saved_inverse.shape[3]
    local_rows = tiles_r * tile_size
    local_cols = tiles_c * tile_size
    w_local = saved_inverse.reshape(local_rows, local_cols)
    adj_local = inverse_adjoint.reshape(local_rows, local_cols)
    row_pos = jnp.arange(local_rows, dtype=jnp.int32)
    col_pos = jnp.arange(local_cols, dtype=jnp.int32)
    row_global = (row_pos // tile_size * row_count + row_at) * tile_size + row_pos % tile_size
    col_global = (col_pos // tile_size * col_count + col_at) * tile_size + col_pos % tile_size
    w_masked = jnp.where(col_global[None, :] <= row_global[:, None], w_local, 0.0)
    start_tile = M // 2 // (tile_size * row_count)
    pieces = []
    for panel_tile in range(K // tile_size):
        owner_row = panel_tile % row_count
        tile_block = start_tile + panel_tile // row_count
        pieces.append(
            jnp.where(
                row_at == owner_row,
                w_masked[tile_block * tile_size : (tile_block + 1) * tile_size],
                0.0,
            )
        )
    panel_data = lax.psum(jnp.concatenate(pieces, 0), "row")
    shared_part = lax.psum_scatter(
        lax.dot_general(
            adj_local,
            panel_data,
            (((1,), (1,)), ((), ())),
            precision=lax.Precision.HIGHEST,
            preferred_element_type=jnp.float32,
        ),
        "col",
        scatter_dimension=0,
        tiled=True,
    )
    partial_sum = lax.dot_general(
        lax.all_gather(shared_part, "col", axis=0, tiled=True),
        w_masked,
        (((0,), (0,)), ((), ())),
        precision=lax.Precision.HIGHEST,
        preferred_element_type=jnp.float32,
    )
    owned_part = lax.psum_scatter(partial_sum, "row", scatter_dimension=0, tiled=True)
    kept = K // row_count
    panel_col = row_at * kept + jnp.arange(kept, dtype=jnp.int32)
    result = jnp.where(col_global[None, :] >= M // 2 + panel_col[:, None], -owned_part, 0.0)
    return result.reshape(kept, tiles_c, 1, tile_size)


def solution(mesh):
    placed = (P(None, "row", None, None, "col", None), P(None, "row", None, None, "col", None))
    return jax.shard_map(
        per_device,
        mesh=mesh,
        in_specs=placed,
        out_specs=P("row", None, "col", None),
        check_vma=False,
    )
```

profile of v0, /device:TPU:32, one launch (start us, length us, event | category | flops | bytes accessed | tf_op | source)
XLA Modules:
  0.0 489.0 jit_solution(2112618393804219557)
XLA Ops:
  6.5 0.0 all-reduce.2.cloned.1.call-start
  6.6 2.7 copy.8
  9.2 0.8 bitcast_select_fusion
  10.0 0.0 copy-start
  10.0 1.9 copy-done
  11.9 0.3 slice_select_fusion.1
  12.3 1.5 pad_maximum_fusion
  13.8 0.0 all-reduce.2.cloned.1.call-update
  13.8 0.0 reduce-scatter.7.cloned.1.call-start
  13.8 4.6 copy.9
  18.4 108.5 %all-reduce.2.cloned.1.call-done = f32[1024,512]{1,0:T(8,128)} async-done(((f32[1024,512]{1,0:T(8,128)}), f32[1024,512]{1,0:T(8,128)}) %all-reduce.2.cloned.1.call-update) | async-done | bytes 2097168 | tf_op jit(solution)/shard_map/psum | solution.py:39
  126.9 18.0 %convolution_bitcast_fusion = f32[2048,1024]{0,1:T(8,128)} fusion(f32[1024,512]{1,0:T(8,128)} %all-reduce.2.cloned.1.call-done, f32[2048,512]{1,0:T(8,128)} %bitcast.12), kind=kOutput, calls=%fused_computation | convolution fusion | flops 12884901888 | bytes 14680064 | tf_op jit(solution)/shard_map/dot_general | solution.py:41
  144.9 9.3 %copy.6 = f32[2048,1024]{1,0:T(8,128)} copy(f32[2048,1024]{0,1:T(8,128)} %convolution_bitcast_fusion) | data formatting | bytes 16777216
  154.2 0.0 reduce-scatter.7.cloned.1.call-update
  154.2 0.0 all-gather.2.cloned.1.call-start
  154.2 153.4 %reduce-scatter.7.cloned.1.call-done = f32[64,1024]{1,0:T(8,128)} async-done(((f32[2048,1024]{1,0:T(8,128)}), f32[64,1024]{1,0:T(8,128)}) %reduce-scatter.7.cloned.1.call-update) | async-done | bytes 262160 | tf_op jit(solution)/shard_map/reduce_scatter | solution.py:40
  307.6 0.0 all-gather.2.cloned.1.call-update
  307.6 0.2 reduce-scatter.5.cloned.1.call-start
  307.9 102.7 %all-gather.2.cloned.1.call-done = f32[2048,1024]{1,0:T(8,128)} async-done(((f32[64,1024]{1,0:T(8,128)}), f32[2048,1024]{1,0:T(8,128)}) %all-gather.2.cloned.1.call-update) | async-done | bytes 8388624 | tf_op jit(solution)/shard_map/all_gather | solution.py:53
  410.5 18.0 %fusion.22 = f32[1024,512]{1,0:T(8,128)} fusion(f32[2048,1024]{1,0:T(8,128)} %all-gather.2.cloned.1.call-done, f32[2048,512]{1,0:T(8,128)} %copy-done), kind=kOutput, calls=%fused_computation.37 | convolution fusion | flops 12884901888 | bytes 14680064 | tf_op jit(solution)/shard_map/dot_general | solution.py:52
  428.5 0.0 reduce-scatter.5.cloned.1.call-update
  428.6 51.9 %reduce-scatter.5.cloned.1.call-done = f32[128,512]{1,0:T(8,128)} async-done(((f32[1024,512]{1,0:T(8,128)}), f32[128,512]{1,0:T(8,128)}) %reduce-scatter.5.cloned.1.call-update) | async-done | bytes 262160 | tf_op jit(solution)/shard_map/reduce_scatter | solution.py:59
  480.5 1.0 select_bitcast_fusion
  481.5 1.0 copy.5
  (3 shorter events, 0.0 us)
Async XLA Ops:
  6.5 120.4 %all-reduce.2.cloned.1.call-start = ((), (), s32[]{:S(2)}) async-start(), calls=%async_computation.2 | async-start | bytes 4194304 | tf_op jit(solution)/shard_map/psum | solution.py:39
  10.0 1.9 copy-start
  13.8 293.8 %reduce-scatter.7.cloned.1.call-start = ((), (), s32[]{:S(2)}) async-start(), calls=%async_computation.5 | async-start | bytes 8650752 | tf_op jit(solution)/shard_map/reduce_scatter | solution.py:40
  154.2 256.4 %all-gather.2.cloned.1.call-start = ((), (), s32[]{:S(2)}) async-start(), calls=%async_computation.3 | async-start | bytes 8650752 | tf_op jit(solution)/shard_map/all_gather | solution.py:53
  307.6 172.8 %reduce-scatter.5.cloned.1.call-start = ((), (), s32[]{:S(2)}) async-start(), calls=%async_computation.4 | async-start | bytes 2359296 | tf_op jit(solution)/shard_map/reduce_scatter | solution.py:59
Sparse Core Ops, SparseCore 0:
  13.9 112.9 all-reduce.1
  154.3 153.2 reduce-scatter.6
  310.4 100.0 all-gather.1
  428.7 51.7 reduce-scatter.4
where the time goes:
time: 489 us
  waiting for transfers between devices  417 us (85%)
  matrix products  36 us (7%)
  local copies, waits for them, and re-layouts  19.4 us (4%)
  between operations  13.2 us (3%)
    reduce_scatter x1, waiting for transfers between devices, per_device(): lax.psum_scatter(lax.dot_general(adj_local, panel_data, (((1,), (1,)), ((...  153 us
    psum x1, waiting for transfers between devices, per_device(): panel_data = lax.psum(jnp.concatenate(pieces, 0), 'row')  108 us
    all_gather x1, waiting for transfers between devices, per_device(): lax.all_gather(shared_part, 'col', axis=0, tiled=True)  103 us
    reduce_scatter x1, waiting for transfers between devices, per_device(): lax.psum_scatter(partial_sum, 'row', scatter_dimension=0, tiled=True)  51.9 us
    unnamed x5, local copies, waits for them, and re-layouts  18.5 us
    dot_general x1, matrix products, per_device(): lax.dot_general(lax.all_gather(shared_part, 'col', axis=0, tiled=True), w...  18 us
    dot_general x1, matrix products, per_device(): lax.dot_general(adj_local, panel_data, (((1,), (1,)), ((), ())), precisio...  18 us
  transfers between devices with their start and end apart: 4, of which 4 were waited for; matrix products, arithmetic and copies ran while one was open for 1% of the time, Pallas kernels for 0%

commit v1 on v0

--- a/solution.py
+++ b/solution.py
@@ -36,7 +36,7 @@
                 0.0,
             )
         )
-    panel_data = lax.psum(jnp.concatenate(pieces, 0), "row")
+    panel_data = jnp.sum(lax.all_gather(jnp.concatenate(pieces, 0), "row"), axis=0)
     shared_part = lax.psum_scatter(
         lax.dot_general(
             adj_local,

time: 489 us -> 717 us (1.47)
  waiting for transfers between devices: 417 us -> 636 us
  other arithmetic: 3.63 us -> 11.7 us
    all_gather x0 -> x1, waiting for transfers between devices: none -> 326 us  [per_device(): lax.all_gather(jnp.concatenate(pieces, 0), 'row')]
    psum x1 -> x0, waiting for transfers between devices: 108 us -> none  [per_device(): panel_data = lax.psum(jnp.concatenate(pieces, 0), 'row')]
    reduce_sum x0 -> x1, other arithmetic: none -> 8.08 us  [per_device(): jnp.sum(lax.all_gather(jnp.concatenate(pieces, 0), 'row'), axis=0)]
where the time goes in v1:
time: 717 us; the launch traced here: 716 us
  waiting for transfers between devices  636 us (89%)
  matrix products  35.3 us (5%)
  local copies, waits for them, and re-layouts  19.4 us (3%)
  between operations  13.2 us (2%)
  other arithmetic  11.7 us (2%)
    all_gather x1, waiting for transfers between devices, per_device(): lax.all_gather(jnp.concatenate(pieces, 0), 'row')  326 us
    reduce_scatter x1, waiting for transfers between devices, per_device(): lax.psum_scatter(lax.dot_general(adj_local, panel_data, (((1,), (1,)), ((...  155 us
    all_gather x1, waiting for transfers between devices, per_device(): lax.all_gather(shared_part, 'col', axis=0, tiled=True)  103 us
    reduce_scatter x1, waiting for transfers between devices, per_device(): lax.psum_scatter(partial_sum, 'row', scatter_dimension=0, tiled=True)  51.9 us
    unnamed x5, local copies, waits for them, and re-layouts  18.5 us
    dot_general x1, matrix products, per_device(): lax.dot_general(lax.all_gather(shared_part, 'col', axis=0, tiled=True), w...  18 us
    dot_general x1, matrix products, per_device(): lax.dot_general(adj_local, panel_data, (((1,), (1,)), ((), ())), precisio...  17.4 us
  transfers between devices with their start and end apart: 4, of which 4 were waited for; matrix products, arithmetic and copies ran while one was open for 1% of the time, Pallas kernels for 0%

profile of v1, /device:TPU:32, one launch (start us, length us, event | category | flops | bytes accessed | tf_op | source)
XLA Modules:
  0.0 715.7 jit_solution(1194991251211377336)
XLA Ops:
  6.5 0.0 all-gather.6.cloned.1.call-start
  6.6 2.7 copy.8
  9.2 0.8 bitcast_select_fusion
  10.0 0.0 copy-start
  10.0 1.9 copy-done
  11.9 0.3 slice_select_fusion.1
  12.3 1.5 pad_maximum_fusion
  13.8 0.0 all-gather.6.cloned.1.call-update
  13.8 0.0 reduce-scatter.7.cloned.1.call-start
  13.9 4.6 copy.9
  18.5 326.2 %all-gather.6.cloned.1.call-done = f32[8192,512]{1,0:T(8,128)} async-done(((f32[1024,512]{1,0:T(8,128)}), f32[8192,512]{1,0:T(8,128)}) %all-gather.6.cloned.1.call-update) | async-done | bytes 16777232 | tf_op jit(solution)/shard_map/all_gather | solution.py:39
  344.7 8.1 %reduce_sum.9 = f32[1024,512]{1,0:T(8,128)S(1)} reduce(f32[8,1024,512]{2,1,0:T(8,128)} %bitcast.13, f32[]{:T(128)} %constant.73.clone.1), dimensions={0}, to_apply=%region_0.1 | reduce | flops 3670016 | bytes 18874372 | tf_op jit(solution)/shard_map/reduce_sum | solution.py:39
  352.8 17.4 %convolution_bitcast_fusion = f32[2048,1024]{0,1:T(8,128)} fusion(f32[1024,512]{1,0:T(8,128)S(1)} %reduce_sum.9, f32[2048,512]{1,0:T(8,128)} %bitcast.14), kind=kOutput, calls=%fused_computation | convolution fusion | flops 12884901888 | bytes 14680064 | tf_op jit(solution)/shard_map/dot_general | solution.py:41
  370.2 9.3 %copy.6 = f32[2048,1024]{1,0:T(8,128)} copy(f32[2048,1024]{0,1:T(8,128)} %convolution_bitcast_fusion) | data formatting | bytes 16777216
  379.4 0.0 reduce-scatter.7.cloned.1.call-update
  379.5 0.0 all-gather.4.cloned.1.call-start
  379.5 154.8 %reduce-scatter.7.cloned.1.call-done = f32[64,1024]{1,0:T(8,128)} async-done(((f32[2048,1024]{1,0:T(8,128)}), f32[64,1024]{1,0:T(8,128)}) %reduce-scatter.7.cloned.1.call-update) | async-done | bytes 262160 | tf_op jit(solution)/shard_map/reduce_scatter | solution.py:40
  534.3 0.0 all-gather.4.cloned.1.call-update
  534.3 0.2 reduce-scatter.5.cloned.1.call-start
  534.5 102.7 %all-gather.4.cloned.1.call-done = f32[2048,1024]{1,0:T(8,128)} async-done(((f32[64,1024]{1,0:T(8,128)}), f32[2048,1024]{1,0:T(8,128)}) %all-gather.4.cloned.1.call-update) | async-done | bytes 8388624 | tf_op jit(solution)/shard_map/all_gather | solution.py:53
  637.2 18.0 %fusion.22 = f32[1024,512]{1,0:T(8,128)} fusion(f32[2048,1024]{1,0:T(8,128)} %all-gather.4.cloned.1.call-done, f32[2048,512]{1,0:T(8,128)} %copy-done), kind=kOutput, calls=%fused_computation.37 | convolution fusion | flops 12884901888 | bytes 14680064 | tf_op jit(solution)/shard_map/dot_general | solution.py:52
  655.2 0.0 reduce-scatter.5.cloned.1.call-update
  655.3 51.9 %reduce-scatter.5.cloned.1.call-done = f32[128,512]{1,0:T(8,128)} async-done(((f32[1024,512]{1,0:T(8,128)}), f32[128,512]{1,0:T(8,128)}) %reduce-scatter.5.cloned.1.call-update) | async-done | bytes 262160 | tf_op jit(solution)/shard_map/reduce_scatter | solution.py:59
  707.2 1.0 select_bitcast_fusion
  708.2 1.0 copy.5
  (3 shorter events, 0.0 us)
Async XLA Ops:
  6.5 338.2 %all-gather.6.cloned.1.call-start = ((), (), s32[]{:S(2)}) async-start(), calls=%async_computation.4 | async-start | bytes 18874368 | tf_op jit(solution)/shard_map/all_gather | solution.py:39
  10.0 1.9 copy-start
  13.8 520.5 %reduce-scatter.7.cloned.1.call-start = ((), (), s32[]{:S(2)}) async-start(), calls=%async_computation.5 | async-start | bytes 8650752 | tf_op jit(solution)/shard_map/reduce_scatter | solution.py:40
  379.5 257.8 %all-gather.4.cloned.1.call-start = ((), (), s32[]{:S(2)}) async-start(), calls=%async_computation.2 | async-start | bytes 8650752 | tf_op jit(solution)/shard_map/all_gather | solution.py:53
  534.3 172.9 %reduce-scatter.5.cloned.1.call-start = ((), (), s32[]{:S(2)}) async-start(), calls=%async_computation.3 | async-start | bytes 2359296 | tf_op jit(solution)/shard_map/reduce_scatter | solution.py:59
Sparse Core Ops, SparseCore 0:
  13.9 330.7 all-gather.5
  379.6 154.6 reduce-scatter.6
  537.1 100.1 all-gather.3
  655.4 51.7 reduce-scatter.4
